TPU v7x, 32 devices: a whole 2x2x4 slice. The times are simulated.
32 devices in a mesh: groups: 2 (over y), seq: 4 (over z), dp: 2 (over x), mp: 2 (over core).
Axes of the slice: x: 2, y: 2, z: 4, core: 2. Of those that a mesh axis runs over, the one named last changes fastest.
Arguments:
- queries: bfloat16 [4, 512, 2048], P(('groups', 'dp'), 'seq', 'mp'), parts along dimension 0, may hold values from -6 to 6
- keys: bfloat16 [4, 512, 2048], P(('groups', 'dp'), 'seq', 'mp'), parts along dimension 0, may hold values from -6 to 6
- values: bfloat16 [4, 512, 2048], P(('groups', 'dp'), 'seq', 'mp'), parts along dimension 0, may hold values from -6 to 6
- grad_output: bfloat16 [4, 512, 2048], P(('groups', 'dp'), 'seq', 'mp'), parts along dimension 0, may hold values from -6 to 6
- counts: int32 [4, 4, 4], P(('groups', 'dp'), 'seq'), parts along dimension 0, may hold values from 0 to 64, as said below
Outputs:
- grad_queries: bfloat16 [4, 512, 2048], P(('groups', 'dp'), 'seq', 'mp'), parts along dimension 0
- grad_keys: bfloat16 [4, 512, 2048], P(('groups', 'dp'), 'seq', 'mp'), parts along dimension 0
- grad_values: bfloat16 [4, 512, 2048], P(('groups', 'dp'), 'seq', 'mp'), parts along dimension 0
There are 2 independent parts, one for each index of `groups`. A program takes and returns all parts, laid end to end along the dimension named above; each array names one. Nothing has to cross between parts.
Inputs may be any that keep to these rules, and one draw needn't show every extreme that they name: Each shard's counts sum to 128; no entry exceeds 64, some window receives 64 points from every shard.
All inputs are finite; a program needn't handle non-finite values.
Results may differ from a plain program's by a relative error of at most 0.001.
Values may be sent and summed in bfloat16 or wider, within the bound.
A program may use at most 128 MiB of HBM per device.

v0:
```python
import math

import jax
import jax.numpy as jnp
from jax import lax
from jax.sharding import PartitionSpec as P

DH = 128


highest = lax.Precision.HIGHEST


def entering(value, axis, join, neutral, backward):
    count, mine = (lax.axis_size(axis), lax.axis_index(axis))
    pieces = lax.all_gather(value, axis)
    if backward:
        pieces = pieces[::-1]
        mine = count - 1 - mine
    total = jnp.full_like(value, 0) + jnp.asarray(neutral, value.dtype)

    def hop(position, total):
        longer = join(total, pieces[position])
        return jnp.where(position < mine, longer, total)

    return lax.fori_loop(0, count - 1, hop, total)


def add_states(earlier, later):
    return earlier + later


def per_device(queries, keys, values, grad_output, counts):
    shard_count = lax.axis_size("seq")
    local_rows = queries.shape[1]
    width = queries.shape[2]
    local_heads = width // DH
    capacity = 2 * local_rows // shard_count
    window_rows = shard_count * capacity
    factor = 1.0 / math.sqrt(DH * local_rows * shard_count)
    my_counts = counts[0, 0]
    window_ends = jnp.cumsum(my_counts)
    window_starts = window_ends - my_counts
    offsets = jnp.arange(capacity, dtype=jnp.int32)
    occupied = offsets[None, :] < my_counts[:, None]
    picked = jnp.where(occupied, window_starts[:, None] + offsets[None, :], 0).reshape(-1)
    occupied_column = occupied.reshape(-1, 1)

    def pack(source):
        taken = jnp.take(source[0], picked, axis=0)
        taken = jnp.where(occupied_column, taken, jnp.zeros_like(taken))
        return taken.reshape(shard_count, capacity, width)

    def split_heads(received):
        return received.reshape(window_rows, local_heads, DH)

    def outer_sum(left, right):
        return jnp.einsum("lha,lhb->hab", left, right, preferred_element_type=jnp.float32)

    query_recv, key_recv, value_recv, grad_recv = (
        lax.all_to_all(pack(queries), "seq", split_axis=0, concat_axis=0, tiled=True),
        lax.all_to_all(pack(keys), "seq", split_axis=0, concat_axis=0, tiled=True),
        lax.all_to_all(pack(values), "seq", split_axis=0, concat_axis=0, tiled=True),
        lax.all_to_all(pack(grad_output), "seq", split_axis=0, concat_axis=0, tiled=True),
    )
    query_recv = split_heads(query_recv)
    key_recv = split_heads(key_recv)
    value_recv = split_heads(value_recv)
    grad_recv = split_heads(grad_recv)
    key_state = outer_sum(key_recv, value_recv)
    query_state = outer_sum(query_recv, grad_recv)
    zero_state = jnp.zeros((local_heads, DH, DH), jnp.float32)
    before_kv = entering(key_state, "seq", add_states, zero_state, False)
    after_qd = entering(query_state, "seq", add_states, zero_state, True)
    block = min(512, window_rows)
    nblocks = window_rows // block

    def blocked(received):
        return received.reshape(nblocks, block, local_heads, DH)

    query_blocks = blocked(query_recv)
    key_blocks = blocked(key_recv)
    value_blocks = blocked(value_recv)
    grad_blocks = blocked(grad_recv)
    block_kv = jnp.einsum(
        "nlha,nlhb->nhab", key_blocks, value_blocks, preferred_element_type=jnp.float32
    )
    block_qd = jnp.einsum(
        "nlha,nlhb->nhab", query_blocks, grad_blocks, preferred_element_type=jnp.float32
    )
    kv_before = before_kv[None] + jnp.cumsum(block_kv, axis=0) - block_kv
    qd_after = after_qd[None] + jnp.sum(block_qd, axis=0)[None] - jnp.cumsum(block_qd, axis=0)
    lower = (
        lax.broadcasted_iota(jnp.int32, (block, block), 0)
        >= lax.broadcasted_iota(jnp.int32, (block, block), 1)
    ).astype(jnp.float32)

    def one_block(pieces):
        query_part, key_part, value_part, grad_part, kv_state, qd_state = pieces
        weights = (
            jnp.einsum("rha,sha->hrs", grad_part, value_part, preferred_element_type=jnp.float32)
            * lower[None]
        )
        scores = (
            jnp.einsum("rha,sha->hrs", query_part, key_part, preferred_element_type=jnp.float32)
            * lower[None]
        )
        query_f = query_part.astype(jnp.float32)
        key_f = key_part.astype(jnp.float32)
        value_f = value_part.astype(jnp.float32)
        grad_f = grad_part.astype(jnp.float32)
        grad_q = jnp.einsum("rhb,hab->rha", grad_f, kv_state, precision=highest) + jnp.einsum(
            "hrs,sha->rha", weights, key_f, precision=highest
        )
        grad_k = jnp.einsum("shb,hab->sha", value_f, qd_state, precision=highest) + jnp.einsum(
            "hrs,rha->sha", weights, query_f, precision=highest
        )
        grad_v = jnp.einsum("sha,hab->shb", key_f, qd_state, precision=highest) + jnp.einsum(
            "hrs,rhb->shb", scores, grad_f, precision=highest
        )

        def finish(result):
            return (result * factor).astype(jnp.bfloat16).reshape(block, width)

        return (finish(grad_q), finish(grad_k), finish(grad_v))

    out_q, out_k, out_v = lax.map(
        one_block, (query_blocks, key_blocks, value_blocks, grad_blocks, kv_before, qd_after)
    )

    def to_slots(result):
        return result.reshape(shard_count, capacity, width)

    back_q, back_k, back_v = (
        lax.all_to_all(to_slots(out_q), "seq", split_axis=0, concat_axis=0, tiled=True),
        lax.all_to_all(to_slots(out_k), "seq", split_axis=0, concat_axis=0, tiled=True),
        lax.all_to_all(to_slots(out_v), "seq", split_axis=0, concat_axis=0, tiled=True),
    )
    positions = jnp.arange(local_rows, dtype=jnp.int32)
    member = (
        (positions[:, None] >= window_starts[None, :]) & (positions[:, None] < window_ends[None, :])
    ).astype(jnp.int32)
    window_of = jnp.sum(member * jnp.arange(shard_count, dtype=jnp.int32)[None, :], axis=1)
    start_of = jnp.sum(member * window_starts[None, :], axis=1)
    source_index = window_of * capacity + positions - start_of

    def unpack(returned):
        return jnp.take(returned.reshape(window_rows, width), source_index, axis=0)[None]

    return (unpack(back_q), unpack(back_k), unpack(back_v))


def solution(mesh):
    placed = (
        P(("groups", "dp"), "seq", "mp"),
        P(("groups", "dp"), "seq", "mp"),
        P(("groups", "dp"), "seq", "mp"),
        P(("groups", "dp"), "seq", "mp"),
        P(("groups", "dp"), "seq", None),
    )
    return jax.shard_map(
        per_device,
        mesh=mesh,
        in_specs=placed,
        out_specs=(
            P(("groups", "dp"), "seq", "mp"),
            P(("groups", "dp"), "seq", "mp"),
            P(("groups", "dp"), "seq", "mp"),
        ),
        check_vma=False,
    )
```

profile of v0, /device:TPU:0, one launch (start us, length us, event | category | flops | bytes accessed | tf_op | source)
XLA Modules:
  0.0 218.9 jit_solution(3963657289021872831)
XLA Ops:
  15.8 20.6 %all_to_all.35 = bf16[4,64,1024]{2,1,0:T(8,128)(2,1)S(1)} all-to-all(bf16[4,64,1024]{2,1,0:T(8,128)(2,1)S(1)} %bitcast.68), channel_id=1, replica_groups=mesh['groups'=2,'seq'=4,'dp'=2,'mp'=2] {'seq'}, dimensions={0} | all-to-all | bytes 1048576 | tf_op jit(solution)/shard_map/all_to_all | solution.py:64
  36.4 3.5 %all-to-all-start.4 = ((bf16[4,64,1024]{2,1,0:T(8,128)(2,1)}), bf16[4,64,1024]{2,1,0:T(8,128)(2,1)S(1)}, u32[]{:S(2)}, u32[]{:S(2)}) async-start(bf16[4,64,1024]{2,1,0:T(8,128)(2,1)} %bitcast.14), calls=%async_computation.4 | async-start | bytes 1048576 | tf_op jit(solution)/shard_map/all_to_all | solution.py:61
  40.4 13.1 %all-to-all-done.4 = bf16[4,64,1024]{2,1,0:T(8,128)(2,1)S(1)} async-done(((bf16[4,64,1024]{2,1,0:T(8,128)(2,1)}), bf16[4,64,1024]{2,1,0:T(8,128)(2,1)S(1)}, u32[]{:S(2)}, u32[]{:S(2)}) %all-to-all-start.4) | async-done | bytes 524320 | tf_op jit(solution)/shard_map/all_to_all | solution.py:61
  54.8 27.9 %all_to_all.36 = bf16[4,64,1024]{2,1,0:T(8,128)(2,1)S(1)} all-to-all(bf16[4,64,1024]{2,1,0:T(8,128)(2,1)S(1)} %bitcast.67), channel_id=1, replica_groups=mesh['groups'=2,'seq'=4,'dp'=2,'mp'=2] {'seq'}, dimensions={0} | all-to-all | bytes 1048576 | tf_op jit(solution)/shard_map/all_to_all | solution.py:62
  82.7 4.1 %all-to-all-start.1 = ((bf16[4,64,1024]{2,1,0:T(8,128)(2,1)}), bf16[4,64,1024]{2,1,0:T(8,128)(2,1)S(1)}, u32[]{:S(2)}, u32[]{:S(2)}) async-start(bf16[4,64,1024]{2,1,0:T(8,128)(2,1)} %bitcast.6), calls=%async_computation.1 | async-start | bytes 1048576 | tf_op jit(solution)/shard_map/all_to_all | solution.py:63
  87.0 25.5 %all-to-all-done.1 = bf16[4,64,1024]{2,1,0:T(8,128)(2,1)S(1)} async-done(((bf16[4,64,1024]{2,1,0:T(8,128)(2,1)}), bf16[4,64,1024]{2,1,0:T(8,128)(2,1)S(1)}, u32[]{:S(2)}, u32[]{:S(2)}) %all-to-all-start.1) | async-done | bytes 524320 | tf_op jit(solution)/shard_map/all_to_all | solution.py:63
  113.3 2.2 fusion.55
  115.6 1.8 fusion.49
  117.4 3.2 %rev.3 = f32[4,8,128,128]{3,2,1,0:T(8,128)} reverse(f32[4,8,128,128]{3,2,1,0:T(8,128)} %bitcast.69), dimensions={0} | reverse | bytes 4194304 | tf_op jit(solution)/shard_map/rev | solution.py:18
  120.7 3.8 %while.35 = (s32[]{:T(128)}, f32[8,128,128]{2,1,0:T(8,128)S(1)}, s32[]{:T(128)}, f32[4,8,128,128]{3,2,1,0:T(8,128)}, s32[]{:T(128)}, /*index=5*/s32[]{:T(128)}) while((s32[]{:T(128)}, f32[8,128,128]{2,1,0:T(8,128)S(1)}, s32[]{:T(128)}, f32[4,8,128,128]{3,2,1,0:T(8,128)}, s32[]{:T(128)}, /*index=5*/s32[]{:T(128)}) %tuple.75), condition=%wide.region_6.9_spmd.clone, body=%wide.region_5.8_spmd.clone.sunk | while | flops 393220 | bytes 1572965 | solution.py:26
  128.6 4.1 %all-to-all-start.6 = ((bf16[4,64,1024]{2,1,0:T(8,128)(2,1)}), bf16[4,64,1024]{2,1,0:T(8,128)(2,1)}, u32[]{:S(2)}, u32[]{:S(2)}) async-start(bf16[4,64,1024]{2,1,0:T(8,128)(2,1)} %reshape.172), calls=%async_computation.6 | async-start | bytes 1048576 | tf_op jit(solution)/shard_map/all_to_all | solution.py:137
  132.7 1.8 fusion.53
  134.5 1.7 fusion.51
  138.5 2.1 reshape.170
  140.6 21.8 %all-to-all-done.6 = bf16[4,64,1024]{2,1,0:T(8,128)(2,1)} async-done(((bf16[4,64,1024]{2,1,0:T(8,128)(2,1)}), bf16[4,64,1024]{2,1,0:T(8,128)(2,1)}, u32[]{:S(2)}, u32[]{:S(2)}) %all-to-all-start.6) | async-done | bytes 524320 | tf_op jit(solution)/shard_map/all_to_all | solution.py:137
  162.4 4.3 %all-to-all-start.5 = ((bf16[4,64,1024]{2,1,0:T(8,128)(2,1)}), bf16[4,64,1024]{2,1,0:T(8,128)(2,1)}, u32[]{:S(2)}, u32[]{:S(2)}) async-start(bf16[4,64,1024]{2,1,0:T(8,128)(2,1)} %reshape.170), calls=%async_computation.5 | async-start | bytes 1048576 | tf_op jit(solution)/shard_map/all_to_all | solution.py:136
  166.7 17.4 %all-gather.5.cloned.1.call-done = f32[32,128,128]{2,1,0:T(8,128)} async-done(((f32[8,128,128]{2,1,0:T(8,128)}), f32[32,128,128]{2,1,0:T(8,128)}) %all-gather.5.cloned.1.call-update) | async-done | bytes 2097168 | tf_op jit(solution)/shard_map/all_gather | solution.py:16
  184.1 3.8 %while.34 = (s32[]{:T(128)}, f32[8,128,128]{2,1,0:T(8,128)S(1)}, s32[]{:T(128)}, f32[4,8,128,128]{3,2,1,0:T(8,128)}, s32[]{:T(128)}, /*index=5*/s32[]{:T(128)}) while((s32[]{:T(128)}, f32[8,128,128]{2,1,0:T(8,128)S(1)}, s32[]{:T(128)}, f32[4,8,128,128]{3,2,1,0:T(8,128)}, s32[]{:T(128)}, /*index=5*/s32[]{:T(128)}) %tuple.85), condition=%wide.region_2.4_spmd.clone, body=%wide.region_1.3_spmd.clone.sunk | while | flops 393220 | bytes 1572965 | solution.py:26
  187.9 1.7 fusion.45
  189.6 1.4 fusion.33
  192.5 3.5 %all-to-all-start.3 = ((bf16[4,64,1024]{2,1,0:T(8,128)(2,1)}), bf16[4,64,1024]{2,1,0:T(8,128)(2,1)S(1)}, u32[]{:S(2)}, u32[]{:S(2)}) async-start(bf16[4,64,1024]{2,1,0:T(8,128)(2,1)} %reshape.166), calls=%async_computation.3 | async-start | bytes 1048576 | tf_op jit(solution)/shard_map/all_to_all | solution.py:135
  196.0 2.2 gather_fusion.6
  198.2 2.2 gather_fusion.5
  200.4 9.9 %all-to-all-done.3 = bf16[4,64,1024]{2,1,0:T(8,128)(2,1)S(1)} async-done(((bf16[4,64,1024]{2,1,0:T(8,128)(2,1)}), bf16[4,64,1024]{2,1,0:T(8,128)(2,1)S(1)}, u32[]{:S(2)}, u32[]{:S(2)}) %all-to-all-start.3) | async-done | bytes 524320 | tf_op jit(solution)/shard_map/all_to_all | solution.py:135
  (79 shorter events, 28.5 us)
Async XLA Ops:
  7.2 2.5 %copy-start = (bf16[1,128,1024]{2,1,0:T(8,128)(2,1)S(1)}, bf16[1,128,1024]{2,1,0:T(8,128)(2,1)}, u32[]{:S(2)}) copy-start(bf16[1,128,1024]{2,1,0:T(8,128)(2,1)} %param.13) | copy-start | bytes 786436
  9.7 1.2 copy-start.1
  10.9 1.2 copy-start.2
  12.1 1.2 copy-start.3
  36.4 17.1 %all-to-all-start.4 = ((bf16[4,64,1024]{2,1,0:T(8,128)(2,1)}), bf16[4,64,1024]{2,1,0:T(8,128)(2,1)S(1)}, u32[]{:S(2)}, u32[]{:S(2)}) async-start(bf16[4,64,1024]{2,1,0:T(8,128)(2,1)} %bitcast.14), calls=%async_computation.4 | async-start | bytes 1048576 | tf_op jit(solution)/shard_map/all_to_all | solution.py:61
  39.9 77.6 %all-gather.7.cloned.1.call-start = ((), (), s32[]{:S(2)}) async-start(), calls=%async_computation.8 | async-start | bytes 2621440 | tf_op jit(solution)/shard_map/all_gather | solution.py:16
  40.3 84.8 %copy-start.4 = (bf16[256,8,128]{0,2,1:T(8,128)(2,1)}, bf16[256,8,128]{0,2,1:T(8,128)(2,1)S(1)}, u32[]{:S(2)}) copy-start(bf16[256,8,128]{0,2,1:T(8,128)(2,1)S(1)} %copy.66) | copy-start | bytes 1572868
  53.6 62.0 %copy-start.10 = (bf16[32,8,8,128]{3,2,1,0:T(8,128)(2,1)}, bf16[32,8,8,128]{3,2,1,0:T(8,128)(2,1)S(1)}, u32[]{:S(2)}) copy-start(bf16[32,8,8,128]{3,2,1,0:T(8,128)(2,1)S(1)} %copy.72) | copy-start | bytes 1572868
  82.7 29.7 %all-to-all-start.1 = ((bf16[4,64,1024]{2,1,0:T(8,128)(2,1)}), bf16[4,64,1024]{2,1,0:T(8,128)(2,1)S(1)}, u32[]{:S(2)}, u32[]{:S(2)}) async-start(bf16[4,64,1024]{2,1,0:T(8,128)(2,1)} %bitcast.6), calls=%async_computation.1 | async-start | bytes 1048576 | tf_op jit(solution)/shard_map/all_to_all | solution.py:63
  86.9 97.3 %all-gather.5.cloned.1.call-start = ((), (), s32[]{:S(2)}) async-start(), calls=%async_computation.7 | async-start | bytes 2621440 | tf_op jit(solution)/shard_map/all_gather | solution.py:16
  87.0 37.5 %copy-start.6 = (bf16[32,8,8,128]{3,2,1,0:T(8,128)(2,1)}, bf16[32,8,8,128]{3,2,1,0:T(8,128)(2,1)S(1)}, u32[]{:S(2)}) copy-start(bf16[32,8,8,128]{3,2,1,0:T(8,128)(2,1)S(1)} %copy.69) | copy-start | bytes 1572868
  115.6 9.5 %copy-start.13 = (f32[256,256]{1,0:T(8,128)}, f32[256,256]{1,0:T(8,128)S(1)}, u32[]{:S(2)}) copy-start(f32[256,256]{1,0:T(8,128)S(1)} %fusion.62) | copy-start | bytes 786436
  120.7 3.9 %copy-start.8 = (f32[8,128,128]{2,1,0:T(8,128)S(1)}, f32[8,128,128]{2,1,0:T(8,128)}, u32[]{:S(2)}) copy-start(f32[8,128,128]{2,1,0:T(8,128)} %fusion.47) | copy-start | bytes 1572868
  124.5 1.7 copy-start.12
  128.6 33.8 %all-to-all-start.6 = ((bf16[4,64,1024]{2,1,0:T(8,128)(2,1)}), bf16[4,64,1024]{2,1,0:T(8,128)(2,1)}, u32[]{:S(2)}, u32[]{:S(2)}) async-start(bf16[4,64,1024]{2,1,0:T(8,128)(2,1)} %reshape.172), calls=%async_computation.6 | async-start | bytes 1048576 | tf_op jit(solution)/shard_map/all_to_all | solution.py:137
  132.7 1.8 copy-start.9
  134.5 1.7 copy-start.11
  134.5 1.7 copy-start.14
  162.4 30.1 %all-to-all-start.5 = ((bf16[4,64,1024]{2,1,0:T(8,128)(2,1)}), bf16[4,64,1024]{2,1,0:T(8,128)(2,1)}, u32[]{:S(2)}, u32[]{:S(2)}) async-start(bf16[4,64,1024]{2,1,0:T(8,128)(2,1)} %reshape.170), calls=%async_computation.5 | async-start | bytes 1048576 | tf_op jit(solution)/shard_map/all_to_all | solution.py:136
  184.1 3.8 %copy-start.5 = (bf16[256,8,128]{0,2,1:T(8,128)(2,1)S(1)}, bf16[256,8,128]{0,2,1:T(8,128)(2,1)}, u32[]{:S(2)}) copy-start(bf16[256,8,128]{0,2,1:T(8,128)(2,1)} %copy-done.4) | copy-start | bytes 1572868
  187.9 1.7 copy-start.7
  187.9 1.7 copy-start.15
  192.5 17.8 %all-to-all-start.3 = ((bf16[4,64,1024]{2,1,0:T(8,128)(2,1)}), bf16[4,64,1024]{2,1,0:T(8,128)(2,1)S(1)}, u32[]{:S(2)}, u32[]{:S(2)}) async-start(bf16[4,64,1024]{2,1,0:T(8,128)(2,1)} %reshape.166), calls=%async_computation.3 | async-start | bytes 1048576 | tf_op jit(solution)/shard_map/all_to_all | solution.py:135
Sparse Core Ops, SparseCore 0:
  54.9 61.5 all-gather.6
  118.1 65.9 all-gather.4
where the time goes:
time: 220 us; the launch traced here: 219 us
  waiting for transfers between devices  87.7 us (40%)
  blocking collectives  48.5 us (22%)
  local copies, waits for them, and re-layouts  21.6 us (10%)
  starting transfers between devices  19.6 us (9%)
  matrix products  14.6 us (7%)
  between operations  14.5 us (7%)
  other arithmetic  12.3 us (6%)
    all_to_all x1, blocking collectives, per_device(): lax.all_to_all(pack(keys), 'seq', split_axis=0, concat_axis=0, tiled=True)  27.9 us
    all_to_all x1, waiting for transfers between devices, per_device(): lax.all_to_all(pack(values), 'seq', split_axis=0, concat_axis=0, tiled=True)  25.5 us
    all_to_all x1, waiting for transfers between devices, per_device(): lax.all_to_all(to_slots(out_v), 'seq', split_axis=0, concat_axis=0, tiled...  21.8 us
    all_to_all x1, blocking collectives, per_device(): lax.all_to_all(pack(grad_output), 'seq', split_axis=0, concat_axis=0, til...  20.6 us
    all_gather x2, waiting for transfers between devices, entering(): pieces = lax.all_gather(value, axis)  17.4 us
    all_to_all x1, waiting for transfers between devices, per_device(): lax.all_to_all(pack(queries), 'seq', split_axis=0, concat_axis=0, tiled=T...  13.1 us
    all_to_all x1, waiting for transfers between devices, per_device(): lax.all_to_all(to_slots(out_q), 'seq', split_axis=0, concat_axis=0, tiled...  9.87 us
    select_n x6, other arithmetic, hop(): return jnp.where(position < mine, longer, total)  7.5 us
  transfers between devices with their start and end apart: 7, of which 5 were waited for; matrix products, arithmetic and copies ran while one was open for 16% of the time, Pallas kernels for 0%

commit v1 on v0

--- a/solution.py
+++ b/solution.py
@@ -1,8 +1,11 @@
+import functools
 import math
 
 import jax
 import jax.numpy as jnp
 from jax import lax
+from jax.experimental import pallas as pl
+from jax.experimental.pallas import tpu as pltpu
 from jax.sharding import PartitionSpec as P
 
 DH = 128
@@ -150,6 +153,247 @@
     return (unpack(back_q), unpack(back_k), unpack(back_v))
 
 
+MESH = pl.DeviceIdType.MESH
+
+
+def exchange_kernel(
+    n,
+    rows,
+    owned,
+    q_ref,
+    k_ref,
+    v_ref,
+    g_ref,
+    counts_ref,
+    dq_ref,
+    dk_ref,
+    dv_ref,
+    held,
+    ends,
+    key_row,
+    key_col,
+    result,
+    in_send,
+    in_recv,
+    own_sem,
+    ends_send,
+    ends_recv,
+    out_send,
+    out_recv,
+    back_sem,
+):
+    me = lax.axis_index("seq")
+    total = n * rows
+    factor = 1.0 / math.sqrt(DH * total)
+    sources = (q_ref, k_ref, v_ref, g_ref)
+    outputs = (dq_ref, dk_ref, dv_ref)
+    peers = [lax.rem(me + d, n) for d in range(n)]
+    senders = [lax.rem(me + n - d, n) for d in range(n)]
+
+    def columns(owner, head):
+        return pl.ds(pl.multiple_of((owner * owned + head) * DH, DH), DH)
+
+    def block(shard):
+        return pl.ds(pl.multiple_of(shard * rows, rows), rows)
+
+    barrier = pltpu.get_barrier_semaphore()
+    for d in range(1, n):
+        pl.semaphore_signal(barrier, inc=1, device_id={"seq": peers[d]}, device_id_type=MESH)
+
+    own = [
+        [
+            pltpu.make_async_copy(
+                sources[t].at[0, :, columns(me, h)], held.at[h, t, block(me)], own_sem.at[h, t]
+            )
+            for t in range(4)
+        ]
+        for h in range(owned)
+    ]
+    for h in range(owned):
+        for t in range(4):
+            own[h][t].start()
+
+    lanes = lax.broadcasted_iota(jnp.int32, (8, 128), 1)
+    end = jnp.zeros((1, 1), jnp.int32)
+    table = jnp.zeros((8, 128), jnp.int32)
+    for w in range(n):
+        end = end + counts_ref[0, 0:1, w : w + 1]
+        table = jnp.where(lanes == w, end, table)
+    ends[me] = table
+
+    pl.semaphore_wait(barrier, n - 1)
+
+    ends_copies = [None]
+    for d in range(1, n):
+        copy = pltpu.make_async_remote_copy(
+            src_ref=ends.at[me],
+            dst_ref=ends.at[me],
+            send_sem=ends_send.at[d],
+            recv_sem=ends_recv.at[d],
+            device_id={"seq": peers[d]},
+            device_id_type=MESH,
+        )
+        copy.start()
+        ends_copies.append(copy)
+
+    in_copies = {}
+    for h in range(owned):
+        for t in range(4):
+            for d in range(1, n):
+                copy = pltpu.make_async_remote_copy(
+                    src_ref=sources[t].at[0, :, columns(peers[d], h)],
+                    dst_ref=held.at[h, t, block(me)],
+                    send_sem=in_send.at[h, t, d],
+                    recv_sem=in_recv.at[h, t, d],
+                    device_id={"seq": peers[d]},
+                    device_id_type=MESH,
+                )
+                copy.start()
+                in_copies[h, t, d] = copy
+
+    def arrive(h, t, d):
+        return pltpu.make_async_remote_copy(
+            src_ref=sources[t].at[0, :, columns(me, h)],
+            dst_ref=held.at[h, t, block(senders[d])],
+            send_sem=in_send.at[h, t, d],
+            recv_sem=in_recv.at[h, t, d],
+            device_id={"seq": peers[d]},
+            device_id_type=MESH,
+        )
+
+    for d in range(1, n):
+        pltpu.make_async_remote_copy(
+            src_ref=ends.at[me],
+            dst_ref=ends.at[senders[d]],
+            send_sem=ends_send.at[d],
+            recv_sem=ends_recv.at[d],
+            device_id={"seq": peers[d]},
+            device_id_type=MESH,
+        ).wait_recv()
+
+    across = lax.broadcasted_iota(jnp.int32, (1, rows), 1)
+    down = lax.broadcasted_iota(jnp.int32, (rows, 128), 0)
+    for s in range(n):
+        window_row = jnp.zeros((1, rows), jnp.int32)
+        window_col = jnp.zeros((rows, 128), jnp.int32)
+        for w in range(n):
+            stop = ends[s, 0:1, w : w + 1]
+            window_row = window_row + jnp.where(across >= stop, 1, 0)
+            window_col = window_col + jnp.where(down >= stop, 1, 0)
+        key_row[0:1, s * rows : (s + 1) * rows] = (window_row * n + s) * rows + across
+        key_col[s] = (window_col * n + s) * rows + down
+
+    def scores(left, right):
+        return lax.dot_general(
+            left, right, (((1,), (1,)), ((), ())), preferred_element_type=jnp.float32
+        )
+
+    def weighted(weights, right):
+        high = weights.astype(jnp.bfloat16)
+        low = (weights - high.astype(jnp.float32)).astype(jnp.bfloat16)
+        product = jnp.dot(high, right, preferred_element_type=jnp.float32) + jnp.dot(
+            low, right, preferred_element_type=jnp.float32
+        )
+        return (product * factor).astype(jnp.bfloat16)
+
+    back_copies = []
+    for h in range(owned):
+        for t in range(4):
+            own[h][t].wait()
+            for d in range(1, n):
+                arrive(h, t, d).wait_recv()
+        for step in range(1, n + 1):
+            d = step % n
+            s = peers[d]
+            col = jnp.concatenate([key_col[s]] * (total // 128), axis=1)
+            row = key_row[...]
+            earlier = row <= col
+            later = row >= col
+            q_all, k_all = (held[h, 0], held[h, 1])
+            v_all, g_all = (held[h, 2], held[h, 3])
+            k_own, v_own = (held[h, 1, block(s), :], held[h, 2, block(s), :])
+            g_own = held[h, 3, block(s), :]
+            result[h, 0, s] = weighted(jnp.where(earlier, scores(g_own, v_all), 0.0), k_all)
+            result[h, 1, s] = weighted(jnp.where(later, scores(v_own, g_all), 0.0), q_all)
+            result[h, 2, s] = weighted(jnp.where(later, scores(k_own, q_all), 0.0), g_all)
+            for t in range(3):
+                if d == 0:
+                    copy = pltpu.make_async_copy(
+                        result.at[h, t, s], outputs[t].at[0, :, columns(me, h)], back_sem.at[h, t]
+                    )
+                else:
+                    copy = pltpu.make_async_remote_copy(
+                        src_ref=result.at[h, t, s],
+                        dst_ref=outputs[t].at[0, :, columns(me, h)],
+                        send_sem=out_send.at[h, t, d],
+                        recv_sem=out_recv.at[h, t, d],
+                        device_id={"seq": s},
+                        device_id_type=MESH,
+                    )
+                copy.start()
+                back_copies.append((d, copy))
+
+    for d in range(1, n):
+        ends_copies[d].wait_send()
+    for copy in in_copies.values():
+        copy.wait_send()
+    for h in range(owned):
+        for d in range(1, n):
+            for t in range(3):
+                pltpu.make_async_remote_copy(
+                    src_ref=result.at[h, t, me],
+                    dst_ref=outputs[t].at[0, :, columns(senders[d], h)],
+                    send_sem=out_send.at[h, t, d],
+                    recv_sem=out_recv.at[h, t, d],
+                    device_id={"seq": peers[d]},
+                    device_id_type=MESH,
+                ).wait_recv()
+    for d, copy in back_copies:
+        if d == 0:
+            copy.wait()
+        else:
+            copy.wait_send()
+
+
+def by_heads(queries, keys, values, grad_output, counts):
+    n = lax.axis_size("seq")
+    rows, width = queries.shape[1:]
+    owned = width // DH // n
+    dma = pltpu.SemaphoreType.DMA
+    anywhere = pl.BlockSpec(memory_space=pl.ANY)
+    return pl.pallas_call(
+        functools.partial(exchange_kernel, n, rows, owned),
+        out_shape=[jax.ShapeDtypeStruct(queries.shape, jnp.bfloat16)] * 3,
+        in_specs=[anywhere] * 4 + [pl.BlockSpec(memory_space=pltpu.VMEM)],
+        out_specs=[anywhere] * 3,
+        scratch_shapes=[
+            pltpu.VMEM((owned, 4, n * rows, DH), jnp.bfloat16),
+            pltpu.VMEM((n, 8, 128), jnp.int32),
+            pltpu.VMEM((1, n * rows), jnp.int32),
+            pltpu.VMEM((n, rows, 128), jnp.int32),
+            pltpu.VMEM((owned, 3, n, rows, DH), jnp.bfloat16),
+            dma((owned, 4, n)),
+            dma((owned, 4, n)),
+            dma((owned, 4)),
+            dma((n,)),
+            dma((n,)),
+            dma((owned, 3, n)),
+            dma((owned, 3, n)),
+            dma((owned, 3)),
+        ],
+        compiler_params=pltpu.CompilerParams(collective_id=0, has_side_effects=True),
+    )(queries, keys, values, grad_output, counts)
+
+
+def per_shard(queries, keys, values, grad_output, counts):
+    n = lax.axis_size("seq")
+    rows, width = queries.shape[1:]
+    heads = width // DH
+    if heads % n == 0 and rows % 128 == 0 and n <= 128:
+        return by_heads(queries, keys, values, grad_output, counts)
+    return per_device(queries, keys, values, grad_output, counts)
+
+
 def solution(mesh):
     placed = (
         P(("groups", "dp"), "seq", "mp"),
@@ -159,7 +403,7 @@
         P(("groups", "dp"), "seq", None),
     )
     return jax.shard_map(
-        per_device,
+        per_shard,
         mesh=mesh,
         in_specs=placed,
         out_specs=(

time: 220 us -> 50.2 us (0.23)
  waiting for transfers between devices: 87.7 us -> 0 us
  blocking collectives: 48.5 us -> 0 us
  Pallas kernels: 0 us -> 45.9 us
  starting transfers between devices: 19.6 us -> 0 us
  local copies, waits for them, and re-layouts: 21.6 us -> 3.46 us
  matrix products: 14.6 us -> 0 us
  between operations: 14.5 us -> 0.65 us
  other arithmetic: 12.3 us -> 0 us
    all_to_all x5 -> x0, waiting for transfers between devices: 70.3 us -> none  [the longest x1 25.5 us: per_device(): lax.all_to_all(pack(values), 'seq', split_axis=0, concat_axis=0, tiled=True)]
    all_to_all x2 -> x0, blocking collectives: 48.5 us -> none  [the longest x1 27.9 us: per_device(): lax.all_to_all(pack(keys), 'seq', split_axis=0, concat_axis=0, tiled=True)]
    pallas_call x0 -> x1, Pallas kernels: none -> 45.9 us  [by_heads(): pl.pallas_call(functools.partial(exchange_kernel, n, rows, owned), out_sh...]
    all_to_all x5 -> x0, starting transfers between devices: 19.5 us -> none  [the longest x1 4.31 us: per_device(): lax.all_to_all(to_slots(out_k), 'seq', split_axis=0, concat_axis=0, tiled...]
    all_gather x2 -> x0, waiting for transfers between devices: 17.4 us -> none  [entering(): pieces = lax.all_gather(value, axis)]
    dot_general x10 -> x0, matrix products: 14.6 us -> none  [the longest x2 3.36 us: outer_sum(): jnp.einsum('lha,lhb->hab', left, right, preferred_element_type=jnp.float32)]
    gather x7 -> x0, local copies, waits for them, and re-layouts: 9.84 us -> none  [the longest x3 5.17 us: unpack(): jnp.take(returned.reshape(window_rows, width), source_index, axis=0)[None]]
    select_n x7 -> x0, other arithmetic: 8.82 us -> none  [the longest x6 7.5 us: hop(): return jnp.where(position < mine, longer, total)]
  transfers between devices with their start and end apart: 7 -> 0, of which waited for: 5 -> 0; matrix products, arithmetic and copies ran while one was open for 16% -> 0% of each run, Pallas kernels for 0% -> 0%
where the time goes in v1:
time: 50.2 us; the launch traced here: 50 us
  Pallas kernels  45.9 us (91%)
  local copies, waits for them, and re-layouts  3.46 us (7%)
  between operations  0.65 us (1%)
    pallas_call x1, Pallas kernels, by_heads(): pl.pallas_call(functools.partial(exchange_kernel, n, rows, owned), out_sh...  45.9 us
    unnamed x7, local copies, waits for them, and re-layouts  3.46 us

profile of v1, /device:TPU:0, one launch (start us, length us, event | category | flops | bytes accessed | tf_op | source)
XLA Modules:
  0.0 50.0 jit_solution(11831777983150306574)
XLA Ops:
  0.6 45.9 %shard_map.76 = (bf16[1,128,1024]{2,1,0:T(8,128)(2,1)}, bf16[1,128,1024]{2,1,0:T(8,128)(2,1)}, bf16[1,128,1024]{2,1,0:T(8,128)(2,1)}) custom-call(bf16[1,128,1024]{2,1,0:T(8,128)(2,1)} %q_ref.1, bf16[1,128,1024]{2,1,0:T(8,128)(2,1)} %k_ref.1, bf16[1,128,1024]{2,1,0:T(8,128)(2,1)} %v_ref.1, bf16[1,128,1024]{2,1,0:T(8,128)(2,1)} %g_ref.1, s32[1,1,4]{2,1,0:T(1,128)} %counts_ref.1), custom_call_target="tpu_custom_call" | custom-call | tf_op jit(solution)/shard_map/pallas_call | solution.py:364
  46.5 0.0 copy-start.1
  46.5 1.7 %copy.11 = bf16[1,128,1024]{2,1,0:T(8,128)(2,1)} copy(bf16[1,128,1024]{2,1,0:T(8,128)(2,1)} %get-tuple-element.6) | data formatting | bytes 524288
  48.2 0.0 copy-done.1
  48.2 0.0 copy-start
  48.2 0.7 %copy.12 = bf16[1,128,1024]{2,1,0:T(8,128)(2,1)} copy(bf16[1,128,1024]{2,1,0:T(8,128)(2,1)S(1)} %copy-done.1) | data formatting | bytes 524288
  49.0 0.3 copy-done
  49.3 0.7 %copy.13 = bf16[1,128,1024]{2,1,0:T(8,128)(2,1)} copy(bf16[1,128,1024]{2,1,0:T(8,128)(2,1)S(1)} %copy-done) | data formatting | bytes 524288
Async XLA Ops:
  46.5 1.7 %copy-start.1 = (bf16[1,128,1024]{2,1,0:T(8,128)(2,1)S(1)}, bf16[1,128,1024]{2,1,0:T(8,128)(2,1)}, u32[]{:S(2)}) copy-start(bf16[1,128,1024]{2,1,0:T(8,128)(2,1)} %get-tuple-element.7) | copy-start | bytes 786436
  48.2 1.0 %copy-start = (bf16[1,128,1024]{2,1,0:T(8,128)(2,1)S(1)}, bf16[1,128,1024]{2,1,0:T(8,128)(2,1)}, u32[]{:S(2)}) copy-start(bf16[1,128,1024]{2,1,0:T(8,128)(2,1)} %get-tuple-element.8) | copy-start | bytes 786436

commit v2 on v1

--- a/solution.py
+++ b/solution.py
@@ -154,6 +154,7 @@
 
 
 MESH = pl.DeviceIdType.MESH
+VMEM_LIMIT = 16 << 20
 
 
 def exchange_kernel(
@@ -169,6 +170,7 @@
     dk_ref,
     dv_ref,
     held,
+    mine,
     ends,
     key_row,
     key_col,
@@ -176,6 +178,7 @@
     in_send,
     in_recv,
     own_sem,
+    mine_sem,
     ends_send,
     ends_recv,
     out_send,
@@ -200,6 +203,8 @@
     for d in range(1, n):
         pl.semaphore_signal(barrier, inc=1, device_id={"seq": peers[d]}, device_id_type=MESH)
 
+    load = pltpu.make_async_copy(counts_ref, mine, mine_sem)
+    load.start()
     own = [
         [
             pltpu.make_async_copy(
@@ -213,11 +218,12 @@
         for t in range(4):
             own[h][t].start()
 
+    load.wait()
     lanes = lax.broadcasted_iota(jnp.int32, (8, 128), 1)
     end = jnp.zeros((1, 1), jnp.int32)
     table = jnp.zeros((8, 128), jnp.int32)
     for w in range(n):
-        end = end + counts_ref[0, 0:1, w : w + 1]
+        end = end + mine[0, 0:1, w : w + 1]
         table = jnp.where(lanes == w, end, table)
     ends[me] = table
 
@@ -355,19 +361,32 @@
             copy.wait_send()
 
 
+def place_kernel(a_ref, b_ref, c_ref, x_ref, y_ref, z_ref, sem):
+    copies = [
+        pltpu.make_async_copy(source, target, sem.at[i])
+        for i, (source, target) in enumerate(((a_ref, x_ref), (b_ref, y_ref), (c_ref, z_ref)))
+    ]
+    for copy in copies:
+        copy.start()
+    for copy in copies:
+        copy.wait()
+
+
 def by_heads(queries, keys, values, grad_output, counts):
     n = lax.axis_size("seq")
     rows, width = queries.shape[1:]
     owned = width // DH // n
     dma = pltpu.SemaphoreType.DMA
     anywhere = pl.BlockSpec(memory_space=pl.ANY)
-    return pl.pallas_call(
+    shapes = [jax.ShapeDtypeStruct(queries.shape, jnp.bfloat16)] * 3
+    gradients = pl.pallas_call(
         functools.partial(exchange_kernel, n, rows, owned),
-        out_shape=[jax.ShapeDtypeStruct(queries.shape, jnp.bfloat16)] * 3,
-        in_specs=[anywhere] * 4 + [pl.BlockSpec(memory_space=pltpu.VMEM)],
+        out_shape=shapes,
+        in_specs=[pl.BlockSpec(memory_space=pltpu.HBM)] * 5,
         out_specs=[anywhere] * 3,
         scratch_shapes=[
             pltpu.VMEM((owned, 4, n * rows, DH), jnp.bfloat16),
+            pltpu.VMEM((1, 1, n), jnp.int32),
             pltpu.VMEM((n, 8, 128), jnp.int32),
             pltpu.VMEM((1, n * rows), jnp.int32),
             pltpu.VMEM((n, rows, 128), jnp.int32),
@@ -375,14 +394,23 @@
             dma((owned, 4, n)),
             dma((owned, 4, n)),
             dma((owned, 4)),
+            dma(()),
             dma((n,)),
             dma((n,)),
             dma((owned, 3, n)),
             dma((owned, 3, n)),
             dma((owned, 3)),
         ],
-        compiler_params=pltpu.CompilerParams(collective_id=0, has_side_effects=True),
-    )(queries, keys, values, grad_output, counts)
+        compiler_params=pltpu.CompilerParams(collective_id=0, has_side_effects=True, vmem_limit_bytes=VMEM_LIMIT),
+    )(*(pltpu.with_memory_space_constraint(x, pltpu.HBM) for x in (queries, keys, values, grad_output, counts)))
+    return pl.pallas_call(
+        place_kernel,
+        out_shape=shapes,
+        in_specs=[anywhere] * 3,
+        out_specs=[anywhere] * 3,
+        scratch_shapes=[dma((3,))],
+        compiler_params=pltpu.CompilerParams(vmem_limit_bytes=VMEM_LIMIT),
+    )(*gradients)
 
 
 def per_shard(queries, keys, values, grad_output, counts):

time: 50.2 us -> 47.4 us (0.944)
  local copies, waits for them, and re-layouts: 3.46 us -> 0 us
  Pallas kernels: 45.9 us -> 46.6 us
    unnamed x7 -> x0, local copies, waits for them, and re-layouts: 3.46 us -> none
    pallas_call x0 -> x1, Pallas kernels: none -> 0.9 us  [by_heads(): pl.pallas_call(place_kernel, out_shape=shapes, in_specs=[anywhere] * 3, o...]
where the time goes in v2:
time: 47.4 us; the launch traced here: 47.2 us
  Pallas kernels  46.6 us (98%)
  between operations  0.64 us (1%)
    pallas_call x1, Pallas kernels, by_heads(): pl.pallas_call(functools.partial(exchange_kernel, n, rows, owned), out_sh...  45.7 us

profile of v2, /device:TPU:0, one launch (start us, length us, event | category | flops | bytes accessed | tf_op | source)
XLA Modules:
  0.0 47.2 jit_solution(11310487332865089425)
XLA Ops:
  0.6 45.7 %shard_map.76 = (bf16[1,128,1024]{2,1,0:T(8,128)(2,1)S(1)}, bf16[1,128,1024]{2,1,0:T(8,128)(2,1)S(1)}, bf16[1,128,1024]{2,1,0:T(8,128)(2,1)S(1)}) custom-call(bf16[1,128,1024]{2,1,0:T(8,128)(2,1)} %q_ref.1, bf16[1,128,1024]{2,1,0:T(8,128)(2,1)} %k_ref.1, bf16[1,128,1024]{2,1,0:T(8,128)(2,1)} %v_ref.1, bf16[1,128,1024]{2,1,0:T(8,128)(2,1)} %g_ref.1, ...), custom_call_target="tpu_custom_call" | custom-call | tf_op jit(solution)/shard_map/pallas_call | solution.py:382
  46.3 0.9 %shard_map.77 = (bf16[1,128,1024]{2,1,0:T(8,128)(2,1)}, bf16[1,128,1024]{2,1,0:T(8,128)(2,1)}, bf16[1,128,1024]{2,1,0:T(8,128)(2,1)}) custom-call(bf16[1,128,1024]{2,1,0:T(8,128)(2,1)S(1)} %get-tuple-element.6.a_ref, bf16[1,128,1024]{2,1,0:T(8,128)(2,1)S(1)} %get-tuple-element.7.b_ref, bf16[1,128,1024]{2,1,0:T(8,128)(2,1)S(1)} %get-tuple-element.8.c_ref), custom_call_target="tpu_custom_call" | custom-call | tf_op jit(solution)/shard_map/pallas_call | solution.py:406

commit v3 on v2

--- a/solution.py
+++ b/solution.py
@@ -191,6 +191,7 @@
     sources = (q_ref, k_ref, v_ref, g_ref)
     outputs = (dq_ref, dk_ref, dv_ref)
     peers = [lax.rem(me + d, n) for d in range(n)]
+    order = sorted(range(1, n), key=lambda d: abs(d - n // 2))
     senders = [lax.rem(me + n - d, n) for d in range(n)]
 
     def columns(owner, head):
@@ -245,7 +246,7 @@
     in_copies = {}
     for h in range(owned):
         for t in range(4):
-            for d in range(1, n):
+            for d in order:
                 copy = pltpu.make_async_remote_copy(
                     src_ref=sources[t].at[0, :, columns(peers[d], h)],
                     dst_ref=held.at[h, t, block(me)],
@@ -303,13 +304,30 @@
         return (product * factor).astype(jnp.bfloat16)
 
     back_copies = []
+
+    def give(h, t, d, s):
+        if d == 0:
+            copy = pltpu.make_async_copy(
+                result.at[h, t, s], outputs[t].at[0, :, columns(me, h)], back_sem.at[h, t]
+            )
+        else:
+            copy = pltpu.make_async_remote_copy(
+                src_ref=result.at[h, t, s],
+                dst_ref=outputs[t].at[0, :, columns(me, h)],
+                send_sem=out_send.at[h, t, d],
+                recv_sem=out_recv.at[h, t, d],
+                device_id={"seq": s},
+                device_id_type=MESH,
+            )
+        copy.start()
+        back_copies.append((d, copy))
+
     for h in range(owned):
         for t in range(4):
             own[h][t].wait()
             for d in range(1, n):
                 arrive(h, t, d).wait_recv()
-        for step in range(1, n + 1):
-            d = step % n
+        for d in order + [0]:
             s = peers[d]
             col = jnp.concatenate([key_col[s]] * (total // 128), axis=1)
             row = key_row[...]
@@ -320,24 +338,11 @@
             k_own, v_own = (held[h, 1, block(s), :], held[h, 2, block(s), :])
             g_own = held[h, 3, block(s), :]
             result[h, 0, s] = weighted(jnp.where(earlier, scores(g_own, v_all), 0.0), k_all)
+            give(h, 0, d, s)
             result[h, 1, s] = weighted(jnp.where(later, scores(v_own, g_all), 0.0), q_all)
+            give(h, 1, d, s)
             result[h, 2, s] = weighted(jnp.where(later, scores(k_own, q_all), 0.0), g_all)
-            for t in range(3):
-                if d == 0:
-                    copy = pltpu.make_async_copy(
-                        result.at[h, t, s], outputs[t].at[0, :, columns(me, h)], back_sem.at[h, t]
-                    )
-                else:
-                    copy = pltpu.make_async_remote_copy(
-                        src_ref=result.at[h, t, s],
-                        dst_ref=outputs[t].at[0, :, columns(me, h)],
-                        send_sem=out_send.at[h, t, d],
-                        recv_sem=out_recv.at[h, t, d],
-                        device_id={"seq": s},
-                        device_id_type=MESH,
-                    )
-                copy.start()
-                back_copies.append((d, copy))
+            give(h, 2, d, s)
 
     for d in range(1, n):
         ends_copies[d].wait_send()

time: 47.4 us -> 47.4 us (level)
  no operation moved by 1% of the time
where the time goes in v3:
time: 47.4 us; the launch traced here: 47.3 us
  Pallas kernels  46.6 us (98%)
  between operations  0.64 us (1%)
    pallas_call x1, Pallas kernels, by_heads(): pl.pallas_call(functools.partial(exchange_kernel, n, rows, owned), out_sh...  45.7 us

profile of v3, /device:TPU:0, one launch (start us, length us, event | category | flops | bytes accessed | tf_op | source)
XLA Modules:
  0.0 47.3 jit_solution(9632274796721975673)
XLA Ops:
  0.6 45.7 %shard_map.76 = (bf16[1,128,1024]{2,1,0:T(8,128)(2,1)S(1)}, bf16[1,128,1024]{2,1,0:T(8,128)(2,1)S(1)}, bf16[1,128,1024]{2,1,0:T(8,128)(2,1)S(1)}) custom-call(bf16[1,128,1024]{2,1,0:T(8,128)(2,1)} %q_ref.1, bf16[1,128,1024]{2,1,0:T(8,128)(2,1)} %k_ref.1, bf16[1,128,1024]{2,1,0:T(8,128)(2,1)} %v_ref.1, bf16[1,128,1024]{2,1,0:T(8,128)(2,1)} %g_ref.1, ...), custom_call_target="tpu_custom_call" | custom-call | tf_op jit(solution)/shard_map/pallas_call | solution.py:387
  46.4 0.9 %shard_map.77 = (bf16[1,128,1024]{2,1,0:T(8,128)(2,1)}, bf16[1,128,1024]{2,1,0:T(8,128)(2,1)}, bf16[1,128,1024]{2,1,0:T(8,128)(2,1)}) custom-call(bf16[1,128,1024]{2,1,0:T(8,128)(2,1)S(1)} %get-tuple-element.6.a_ref, bf16[1,128,1024]{2,1,0:T(8,128)(2,1)S(1)} %get-tuple-element.7.b_ref, bf16[1,128,1024]{2,1,0:T(8,128)(2,1)S(1)} %get-tuple-element.8.c_ref), custom_call_target="tpu_custom_call" | custom-call | tf_op jit(solution)/shard_map/pallas_call | solution.py:411

commit v4 on v2

--- a/solution.py
+++ b/solution.py
@@ -218,32 +218,11 @@
         for t in range(4):
             own[h][t].start()
 
-    load.wait()
-    lanes = lax.broadcasted_iota(jnp.int32, (8, 128), 1)
-    end = jnp.zeros((1, 1), jnp.int32)
-    table = jnp.zeros((8, 128), jnp.int32)
-    for w in range(n):
-        end = end + mine[0, 0:1, w : w + 1]
-        table = jnp.where(lanes == w, end, table)
-    ends[me] = table
-
     pl.semaphore_wait(barrier, n - 1)
 
-    ends_copies = [None]
-    for d in range(1, n):
-        copy = pltpu.make_async_remote_copy(
-            src_ref=ends.at[me],
-            dst_ref=ends.at[me],
-            send_sem=ends_send.at[d],
-            recv_sem=ends_recv.at[d],
-            device_id={"seq": peers[d]},
-            device_id_type=MESH,
-        )
-        copy.start()
-        ends_copies.append(copy)
-
     in_copies = {}
-    for h in range(owned):
+
+    def send_head(h):
         for t in range(4):
             for d in range(1, n):
                 copy = pltpu.make_async_remote_copy(
@@ -256,6 +235,32 @@
                 )
                 copy.start()
                 in_copies[h, t, d] = copy
+
+    send_head(0)
+    load.wait()
+    lanes = lax.broadcasted_iota(jnp.int32, (8, 128), 1)
+    end = jnp.zeros((1, 1), jnp.int32)
+    table = jnp.zeros((8, 128), jnp.int32)
+    for w in range(n):
+        end = end + mine[0, 0:1, w : w + 1]
+        table = jnp.where(lanes == w, end, table)
+    ends[me] = table
+
+    ends_copies = [None]
+    for d in range(1, n):
+        copy = pltpu.make_async_remote_copy(
+            src_ref=ends.at[me],
+            dst_ref=ends.at[me],
+            send_sem=ends_send.at[d],
+            recv_sem=ends_recv.at[d],
+            device_id={"seq": peers[d]},
+            device_id_type=MESH,
+        )
+        copy.start()
+        ends_copies.append(copy)
+
+    for h in range(1, owned):
+        send_head(h)
 
     def arrive(h, t, d):
         return pltpu.make_async_remote_copy(

time: 47.4 us -> 47.1 us (level)
  no operation moved by 1% of the time
where the time goes in v4:
time: 47.1 us; the launch traced here: 46.9 us
  Pallas kernels  46.3 us (98%)
  between operations  0.64 us (1%)
    pallas_call x1, Pallas kernels, by_heads(): pl.pallas_call(functools.partial(exchange_kernel, n, rows, owned), out_sh...  45.4 us

profile of v4, /device:TPU:0, one launch (start us, length us, event | category | flops | bytes accessed | tf_op | source)
XLA Modules:
  0.0 46.9 jit_solution(13938533233126345529)
XLA Ops:
  0.6 45.4 %shard_map.76 = (bf16[1,128,1024]{2,1,0:T(8,128)(2,1)S(1)}, bf16[1,128,1024]{2,1,0:T(8,128)(2,1)S(1)}, bf16[1,128,1024]{2,1,0:T(8,128)(2,1)S(1)}) custom-call(bf16[1,128,1024]{2,1,0:T(8,128)(2,1)} %q_ref.1, bf16[1,128,1024]{2,1,0:T(8,128)(2,1)} %k_ref.1, bf16[1,128,1024]{2,1,0:T(8,128)(2,1)} %v_ref.1, bf16[1,128,1024]{2,1,0:T(8,128)(2,1)} %g_ref.1, ...), custom_call_target="tpu_custom_call" | custom-call | tf_op jit(solution)/shard_map/pallas_call | solution.py:387
  46.0 0.9 %shard_map.77 = (bf16[1,128,1024]{2,1,0:T(8,128)(2,1)}, bf16[1,128,1024]{2,1,0:T(8,128)(2,1)}, bf16[1,128,1024]{2,1,0:T(8,128)(2,1)}) custom-call(bf16[1,128,1024]{2,1,0:T(8,128)(2,1)S(1)} %get-tuple-element.6.a_ref, bf16[1,128,1024]{2,1,0:T(8,128)(2,1)S(1)} %get-tuple-element.7.b_ref, bf16[1,128,1024]{2,1,0:T(8,128)(2,1)S(1)} %get-tuple-element.8.c_ref), custom_call_target="tpu_custom_call" | custom-call | tf_op jit(solution)/shard_map/pallas_call | solution.py:411
